TPU v7x, 512 devices: a whole 4x8x8 slice. The times are simulated.
512 devices in a mesh: grp: 32 (over y, x), tp: 16 (over z, core).
Axes of the slice: x: 4, y: 8, z: 8, core: 2. Of those that a mesh axis runs over, the one named last changes fastest.
Arguments:
- tokens: bfloat16 [65536, 8192], P('grp', 'tp'), may hold values from -6 to 6
- base_weight: bfloat16 [8192, 2048], P('tp'), may hold values from -0.0625 to 0.0625
- down_tables: bfloat16 [4096, 8192, 16], P('grp', 'tp'), may hold values from -0.0625 to 0.0625
- up_tables: bfloat16 [4096, 16, 2048], P('grp', None, 'tp'), may hold values from -1.5 to 1.5
- block_owner: int32 [512, 1], P('grp'), may hold values from 0 to 31; in each aligned block of 16 rows (0 to 15, 16 to 31, ...) at most 2 rows name the same one
- block_local: int32 [512], P('grp'), may hold values from 0 to 127
- block_count: int32 [512], P('grp'), may hold values from 1 to 128
Outputs:
- projected: bfloat16 [65536, 2048], P('grp', 'tp')
Inputs may be any that keep to these rules, and one draw needn't show every extreme that they name: `block_owner`: among the 16 blocks of one group (an aligned run of 16 entries) no owner is named more than 2 times, a bound that some block reaches.
All inputs are finite; a program needn't handle non-finite values.
Results may differ from a plain program's by a relative error of at most 0.001.
Values may be sent and summed in bfloat16 or wider, within the bound.
A program may use at most 64 MiB of HBM per device.

v0:
```python
import jax
import jax.numpy as jnp
from jax import lax
from jax.sharding import PartitionSpec as P

R = 16
BLOCK = 128
CAP = 2


adapter_scale = 2.0


def slot_plan(block_owner):
    owners = block_owner[:, 0]
    block_total = owners.shape[0]
    order = jnp.arange(block_total, dtype=jnp.int32)
    earlier = (owners[None, :] == owners[:, None]) & (order[None, :] < order[:, None])
    ranked = jnp.sum(earlier.astype(jnp.int32), axis=1)
    return owners * CAP + ranked


def body(tokens, base_weight, down_tables, up_tables, block_owner, block_local, block_count):
    group_count = lax.axis_size("grp")
    block_total = block_owner.shape[0]
    feature_cols = tokens.shape[1]
    slot_total = group_count * CAP
    block_slot = slot_plan(block_owner)
    slot_match = block_slot[:, None] == jnp.arange(slot_total, dtype=jnp.int32)[None, :]
    wanted_ids = jnp.sum(jnp.where(slot_match, block_local[:, None], 0), axis=0)
    wanted_ids = wanted_ids.reshape(group_count, CAP)
    partial_value = jnp.dot(tokens, base_weight, preferred_element_type=jnp.float32)
    base_projection = lax.psum_scatter(partial_value, "tp", scatter_dimension=1, tiled=True)
    local_ids = lax.all_to_all(wanted_ids, "grp", split_axis=0, concat_axis=0, tiled=True)
    down_sel = jnp.take(down_tables, local_ids, axis=0)
    up_sel = jnp.take(up_tables, local_ids, axis=0)
    down_got = lax.all_to_all(down_sel, "grp", split_axis=0, concat_axis=0, tiled=True)
    up_got = lax.all_to_all(up_sel, "grp", split_axis=0, concat_axis=0, tiled=True)
    down_block = jnp.take(down_got.reshape(slot_total, feature_cols, R), block_slot, axis=0)
    up_block = jnp.take(up_got.reshape(slot_total, R, up_got.shape[-1]), block_slot, axis=0)
    blocked = tokens.reshape(block_total, BLOCK, feature_cols)
    reduced = jnp.einsum("nbd,ndr->nbr", blocked, down_block, preferred_element_type=jnp.float32)
    reduced = lax.psum(reduced, "tp")
    adapter_output = jnp.einsum(
        "nbr,nro->nbo", reduced, up_block.astype(jnp.float32), precision=lax.Precision.HIGHEST
    )
    row_total = block_total * BLOCK
    adapter_output = adapter_output.reshape(row_total, adapter_output.shape[-1])
    offsets = jnp.arange(BLOCK, dtype=jnp.int32)
    live_rows = (offsets[None, :] < block_count[:, None]).reshape(row_total, 1)
    combined_output = base_projection + adapter_scale * adapter_output
    return jnp.where(live_rows, combined_output, jnp.float32(0.0)).astype(jnp.bfloat16)


def solution(mesh):
    placed = (
        P("grp", "tp"),
        P("tp", None),
        P("grp", "tp", None),
        P("grp", None, "tp"),
        P("grp", None),
        P("grp"),
        P("grp"),
    )
    return jax.shard_map(
        body, mesh=mesh, in_specs=placed, out_specs=P("grp", "tp"), check_vma=False
    )
```

profile of v0, /device:TPU:1, one launch (start us, length us, event | category | flops | bytes accessed | tf_op | source)
XLA Modules:
  0.0 296.7 jit_solution(1352549766239043465)
XLA Ops:
  6.5 0.0 copy-start
  6.5 1.0 convert_reduce_fusion
  7.5 0.7 fusion.12
  8.2 0.7 select_reduce_fusion
  8.9 0.1 all_to_all.16
  9.0 18.9 %all_to_all.25 = s32[32,1,2]{2,1,0:T(1,128)S(1)} all-to-all(s32[32,1,2]{2,1,0:T(1,128)S(1)} %bitcast.46), channel_id=1, replica_groups=mesh['grp'=32,'tp'=16] {'grp'}, dimensions={0} | all-to-all | bytes 512 | tf_op jit(solution)/shard_map/all_to_all | solution.py:34
  28.0 0.1 copy.25
  28.0 0.1 copy.28
  28.1 0.1 reshape.80
  28.3 0.1 copy.26
  28.4 2.2 gather_fusion
  30.6 0.0 copy-start.3
  30.6 1.1 broadcast_select_fusion
  31.7 3.9 %all-to-all-start.1 = ((bf16[32,2,512,16]{2,3,1,0:T(8,128)(2,1)}), bf16[32,2,512,16]{2,3,1,0:T(8,128)(2,1)S(1)}, u32[]{:S(2)}, u32[]{:S(2)}) async-start(bf16[32,2,512,16]{2,3,1,0:T(8,128)(2,1)} %broadcast_select_fusion), calls=%async_computation.2 | async-start | bytes 2097152 | tf_op jit(solution)/shard_map/all_to_all | solution.py:37
  35.7 0.0 all-reduce.2.cloned.1.call-start
  35.7 0.0 copy-done.3
  35.7 25.2 %all-to-all-done.1 = bf16[32,2,512,16]{2,3,1,0:T(8,128)(2,1)S(1)} async-done(((bf16[32,2,512,16]{2,3,1,0:T(8,128)(2,1)}), bf16[32,2,512,16]{2,3,1,0:T(8,128)(2,1)S(1)}, u32[]{:S(2)}, u32[]{:S(2)}) %all-to-all-start.1) | async-done | bytes 1048608 | tf_op jit(solution)/shard_map/all_to_all | solution.py:37
  61.0 0.6 gather_fusion.1
  61.5 0.0 copy-done
  61.6 1.3 convolution_bitcast_fusion
  62.9 0.0 all-reduce.2.cloned.1.call-update
  62.9 0.0 reduce-scatter.2.cloned.1.call-start
  63.0 9.7 %fusion.14 = f32[2048,2048]{1,0:T(8,128)} fusion(bf16[2048,512]{1,0:T(8,128)(2,1)S(1)} %copy-done, bf16[512,2048]{1,0:T(8,128)(2,1)} %param.8), kind=kOutput, calls=%fused_computation.36 | convolution fusion | flops 4294967296 | bytes 20971520 | tf_op jit(solution)/shard_map/dot_general | solution.py:32
  72.7 0.0 copy-start.1
  72.7 0.0 copy-start.2
  72.7 0.0 reduce-scatter.2.cloned.1.call-update
  72.7 1.0 copy-done.1
  73.7 0.6 gather_fusion.2
  74.3 0.8 broadcast_select_fusion.1
  75.2 6.7 %all-to-all-start.2 = ((bf16[32,2,16,128]{3,2,1,0:T(8,128)(2,1)}), bf16[32,2,16,128]{3,2,1,0:T(8,128)(2,1)S(1)}, u32[]{:S(2)}, u32[]{:S(2)}) async-start(bf16[32,2,16,128]{3,2,1,0:T(8,128)(2,1)} %broadcast_select_fusion.1), calls=%async_computation.3 | async-start | bytes 524288 | tf_op jit(solution)/shard_map/all_to_all | solution.py:38
  81.9 0.0 copy-done.2
  81.9 0.1 fusion.8
  82.0 10.3 %all-to-all-done.2 = bf16[32,2,16,128]{3,2,1,0:T(8,128)(2,1)S(1)} async-done(((bf16[32,2,16,128]{3,2,1,0:T(8,128)(2,1)}), bf16[32,2,16,128]{3,2,1,0:T(8,128)(2,1)S(1)}, u32[]{:S(2)}, u32[]{:S(2)}) %all-to-all-start.2) | async-done | bytes 262176 | tf_op jit(solution)/shard_map/all_to_all | solution.py:38
  92.3 0.6 gather_fusion.3
  92.9 89.5 %all-reduce.2.cloned.1.call-done = f32[16,128,16]{1,2,0:T(8,128)} async-done(((f32[16,128,16]{1,2,0:T(8,128)}), f32[16,128,16]{1,2,0:T(8,128)}) %all-reduce.2.cloned.1.call-update) | async-done | bytes 131088 | tf_op jit(solution)/shard_map/psum | solution.py:43
  182.4 1.9 convolution_multiply_fusion
  184.4 103.2 %reduce-scatter.2.cloned.1.call-done = f32[2048,128]{1,0:T(8,128)} async-done(((f32[2048,2048]{1,0:T(8,128)}), f32[2048,128]{1,0:T(8,128)}) %reduce-scatter.2.cloned.1.call-update) | async-done | bytes 1048592 | tf_op jit(solution)/shard_map/reduce_scatter | solution.py:33
  287.5 2.4 fusion.1
  (5 shorter events, 0.0 us)
Async XLA Ops:
  6.5 55.0 %copy-start = (bf16[2048,512]{1,0:T(8,128)(2,1)S(1)}, bf16[2048,512]{1,0:T(8,128)(2,1)}, u32[]{:S(2)}) copy-start(bf16[2048,512]{1,0:T(8,128)(2,1)} %param.7) | copy-start | bytes 6291460
  30.6 5.1 %copy-start.3 = (s32[16,1]{0,1:T(1,128)S(1)}, s32[16,1]{0,1:T(1,128)}, u32[]{:S(2)}) copy-start(s32[16,1]{0,1:T(1,128)} %param.11) | copy-start | bytes 196
  31.7 29.3 %all-to-all-start.1 = ((bf16[32,2,512,16]{2,3,1,0:T(8,128)(2,1)}), bf16[32,2,512,16]{2,3,1,0:T(8,128)(2,1)S(1)}, u32[]{:S(2)}, u32[]{:S(2)}) async-start(bf16[32,2,512,16]{2,3,1,0:T(8,128)(2,1)} %broadcast_select_fusion), calls=%async_computation.2 | async-start | bytes 2097152 | tf_op jit(solution)/shard_map/all_to_all | solution.py:37
  35.7 146.8 %all-reduce.2.cloned.1.call-start = ((), (), s32[]{:S(2)}) async-start(), calls=%async_computation.5 | async-start | bytes 262144 | tf_op jit(solution)/shard_map/psum | solution.py:43
  62.9 224.6 %reduce-scatter.2.cloned.1.call-start = ((), (), s32[]{:S(2)}) async-start(), calls=%async_computation.4 | async-start | bytes 17825792 | tf_op jit(solution)/shard_map/reduce_scatter | solution.py:33
  72.7 1.0 copy-start.1
  72.7 9.3 %copy-start.2 = (s32[16]{0:T(128)S(1)}, s32[16]{0:T(128)}, u32[]{:S(2)}) copy-start(s32[16]{0:T(128)} %param.13) | copy-start | bytes 196
  75.2 17.2 %all-to-all-start.2 = ((bf16[32,2,16,128]{3,2,1,0:T(8,128)(2,1)}), bf16[32,2,16,128]{3,2,1,0:T(8,128)(2,1)S(1)}, u32[]{:S(2)}, u32[]{:S(2)}) async-start(bf16[32,2,16,128]{3,2,1,0:T(8,128)(2,1)} %broadcast_select_fusion.1), calls=%async_computation.3 | async-start | bytes 524288 | tf_op jit(solution)/shard_map/all_to_all | solution.py:38
Sparse Core Ops, SparseCore 0:
  63.0 119.3 all-reduce.1
  185.3 102.2 reduce-scatter.1
where the time goes:
time: 298 us; the launch traced here: 297 us
  waiting for transfers between devices  228 us (77%)
  blocking collectives  18.9 us (6%)
  between operations  13.5 us (5%)
  matrix products  13 us (4%)
  starting transfers between devices  10.7 us (4%)
  other arithmetic  6.85 us (2%)
  local copies, waits for them, and re-layouts  5.47 us (2%)
    reduce_scatter x1, waiting for transfers between devices, body(): lax.psum_scatter(partial_value, 'tp', scatter_dimension=1, tiled=True)  103 us
    psum x1, waiting for transfers between devices, body(): reduced = lax.psum(reduced, 'tp')  89.5 us
    all_to_all x1, waiting for transfers between devices, body(): lax.all_to_all(down_sel, 'grp', split_axis=0, concat_axis=0, tiled=True)  25.2 us
    all_to_all x1, blocking collectives, body(): lax.all_to_all(wanted_ids, 'grp', split_axis=0, concat_axis=0, tiled=True)  18.9 us
    all_to_all x1, waiting for transfers between devices, body(): lax.all_to_all(up_sel, 'grp', split_axis=0, concat_axis=0, tiled=True)  10.3 us
    dot_general x1, matrix products, body(): jnp.dot(tokens, base_weight, preferred_element_type=jnp.float32)  9.68 us
    all_to_all x1, starting transfers between devices, body(): lax.all_to_all(up_sel, 'grp', split_axis=0, concat_axis=0, tiled=True)  6.74 us
  transfers between devices with their start and end apart: 4, of which 4 were waited for; matrix products, arithmetic and copies ran while one was open for 5% of the time, Pallas kernels for 0%

commit v1 on v0

v1 whole, which is shorter than its diff:
```python
import functools

import jax
import jax.numpy as jnp
from jax import lax
from jax.experimental import pallas as pl
from jax.experimental.pallas import tpu as pltpu
from jax.sharding import PartitionSpec as P

R = 16
BLOCK = 128
CAP = 2
COLS = 128
CHUNK = 256
GROUPS = 8
LEVELS = 32766.0
adapter_scale = 2.0

OFFSETS = (4, 0, 3, 5, 2, 6, 1, 7)
PLUS, MINUS = 0, 1


def kernel(
    group_count, tokens, weight, down_table, up_table, owner, local, count, out,
    own_tokens, sib_tokens, own_weight, sib_weight, partial, send_q, recv_q, send_s, recv_s,
    table_d, table_u, send_d, recv_d, send_u, recv_u, id_send, id_recv, id_scalar, slot_scalar,
    rank_part, rank_recv, rank_sum, rank_full,
    load_sem, wload_sem, tok_send, tok_recv, w_send, w_recv, q_send, q_recv, s_send, s_recv,
    id_ssem, id_rsem, copy_sem, d_ssem, d_rsem, u_ssem, u_rsem, r_ssem, r_rsem, f_ssem, f_rsem,
):
    rows, feats = own_tokens.shape
    chunks = rows // CHUNK
    half = chunks // 2
    blocks = rows // BLOCK
    g = lax.axis_index("grp")
    t = lax.axis_index("tp")
    tp = lax.axis_size("tp")
    chips = tp // 2
    z = lax.div(t, 2)
    c = lax.rem(t, 2)
    sibling = 2 * z + 1 - c
    ring = (2 * lax.rem(z + 1, chips) + c, 2 * lax.rem(z + chips - 1, chips) + c)

    barrier = pltpu.get_barrier_semaphore()

    def greet_group(k, carry):
        pl.semaphore_signal(barrier, inc=1, device_id={"grp": lax.rem(g + k, group_count)})
        return carry

    def greet_tp(k, carry):
        pl.semaphore_signal(barrier, inc=1, device_id={"tp": lax.rem(t + k, tp)})
        return carry

    lax.fori_loop(1, group_count, greet_group, 0)
    lax.fori_loop(1, tp, greet_tp, 0)

    load_tokens = pltpu.make_async_copy(tokens, own_tokens, load_sem.at[0])
    load_down = pltpu.make_async_copy(down_table, table_d, load_sem.at[1])
    load_up = pltpu.make_async_copy(up_table, table_u, load_sem.at[2])

    def weight_block(slot, core):
        column = (lax.rem(z + OFFSETS[slot], chips) * 2 + core) * COLS
        return weight.at[:, pl.ds(pl.multiple_of(column, COLS), COLS)]

    load_weight = [
        pltpu.make_async_copy(weight_block(j, c), own_weight.at[:, pl.ds(j * COLS, COLS)], wload_sem.at[j])
        for j in range(8)
    ]
    load_weight[0].start()
    load_weight[1].start()
    load_tokens.start()
    for j in range(2, 8):
        load_weight[j].start()
    load_down.start()
    load_up.start()

    lanes = lax.broadcasted_iota(jnp.int32, (8, 128), 1)
    wanted = jnp.zeros((8, 128), jnp.int32)
    owners = [owner[n] for n in range(blocks)]
    for n in range(blocks):
        earlier = jnp.int32(0)
        for m in range(n):
            earlier = earlier + (owners[m] == owners[n]).astype(jnp.int32)
        slot = owners[n] * CAP + earlier
        slot_scalar[n] = slot
        wanted = jnp.where(lanes == slot, local[n], wanted)
    id_send[...] = wanted
    id_recv[g] = wanted

    pl.semaphore_wait(barrier, group_count - 1 + tp - 1)

    def send_ids(k, carry):
        pltpu.make_async_remote_copy(
            src_ref=id_send, dst_ref=id_recv.at[g], send_sem=id_ssem, recv_sem=id_rsem,
            device_id={"grp": lax.rem(g + k, group_count)},
        ).start()
        return carry

    lax.fori_loop(1, group_count, send_ids, 0)

    def swap_weight(j):
        return pltpu.make_async_remote_copy(
            src_ref=weight_block(j, 1 - c), dst_ref=sib_weight.at[:, pl.ds(j * COLS, COLS)],
            send_sem=w_send.at[j], recv_sem=w_recv.at[j], device_id={"tp": sibling},
        )

    def chunk_rows(r):
        return pl.ds(pl.multiple_of(r * CHUNK, CHUNK), CHUNK)

    def swap_tokens(r):
        return pltpu.make_async_remote_copy(
            src_ref=tokens.at[chunk_rows(r)], dst_ref=sib_tokens.at[chunk_rows(r)],
            send_sem=tok_send.at[r], recv_sem=tok_recv.at[r], device_id={"tp": sibling},
        )

    swap_weight(0).start()
    swap_weight(1).start()
    for i in range(half):
        swap_tokens(i).start()
        swap_tokens(half + i).start()
    for j in range(2, 8):
        swap_weight(j).start()

    def data_copy(d, s, r):
        return pltpu.make_async_remote_copy(
            src_ref=send_q.at[d, s, chunk_rows(r)], dst_ref=recv_q.at[d, s, chunk_rows(r)],
            send_sem=q_send.at[d, s, r], recv_sem=q_recv.at[d, s, r], device_id={"tp": ring[d]},
        )

    def scale_copy(d, s, r):
        return pltpu.make_async_remote_copy(
            src_ref=send_s.at[d, s, r], dst_ref=recv_s.at[d, s, r],
            send_sem=s_send.at[d, s, r], recv_sem=s_recv.at[d, s, r], device_id={"tp": ring[d]},
        )

    def pass_on(d, s, r, value):
        grouped = value.reshape(GROUPS, CHUNK // GROUPS, COLS)
        top = jnp.maximum(jnp.max(jnp.abs(grouped), axis=1), 1e-30)
        send_s[d, s, r] = top * (1.0 / LEVELS)
        coded = jnp.round(grouped * (LEVELS / top)[:, None, :])
        send_q[d, s, chunk_rows(r)] = coded.astype(jnp.int32).astype(jnp.int16).reshape(CHUNK, COLS)
        scale_copy(d, s, r).start()
        data_copy(d, s, r).start()

    def arrived(d, s, r):
        scale_copy(d, s, r).wait_recv()
        data_copy(d, s, r).wait_recv()
        value = recv_q[d, s, chunk_rows(r)].astype(jnp.int32).astype(jnp.float32)
        value = value.reshape(GROUPS, CHUNK // GROUPS, COLS) * recv_s[d, s, r][:, None, :]
        return value.reshape(CHUNK, COLS)

    def product(pair, r):
        columns = pl.ds(pair * 2 * COLS, 2 * COLS)
        return jnp.dot(
            own_tokens[chunk_rows(r)], own_weight[:, columns], preferred_element_type=jnp.float32
        ) + jnp.dot(
            sib_tokens[chunk_rows(r)], sib_weight[:, columns], preferred_element_type=jnp.float32
        )

    load_weight[0].wait()
    load_weight[1].wait()
    load_tokens.wait()
    swap_weight(0).wait_recv()
    swap_weight(1).wait_recv()

    def far_half(d, r):
        swap_tokens(r).wait_recv()
        both = product(0, r)
        partial[1, chunk_rows(r)] = both[:, COLS:]
        pass_on(d, 0, r, both[:, :COLS])

    def far_step(i, carry):
        far_half(PLUS, i)
        far_half(MINUS, half + i)
        return carry

    lax.fori_loop(0, half, far_step, 0)

    all_ids = id_recv.at[pl.ds(0, group_count - 1)]
    pltpu.make_async_copy(all_ids, all_ids, id_rsem).wait()
    fetch_ids = pltpu.make_async_copy(id_recv.at[:, 0], id_scalar, copy_sem)
    fetch_ids.start()
    load_down.wait()
    load_up.wait()
    fetch_ids.wait()

    for r in range(CAP):
        mine = id_scalar[g, CAP * g + r]
        recv_d[CAP * g + r] = table_d[mine]
        recv_u[CAP * g + r] = table_u[mine]

    def pair_of(index):
        return pl.ds(index * CAP, CAP)

    def send_down(k, carry):
        peer = lax.rem(g + k, group_count)
        for r in range(CAP):
            send_d[CAP * peer + r] = table_d[id_scalar[peer, CAP * g + r]]
        pltpu.make_async_remote_copy(
            src_ref=send_d.at[pair_of(peer)], dst_ref=recv_d.at[pair_of(g)],
            send_sem=d_ssem, recv_sem=d_rsem, device_id={"grp": peer},
        ).start()
        return carry

    def send_up(k, carry):
        peer = lax.rem(g + k, group_count)
        for r in range(CAP):
            send_u[CAP * peer + r] = table_u[id_scalar[peer, CAP * g + r]]
        pltpu.make_async_remote_copy(
            src_ref=send_u.at[pair_of(peer)], dst_ref=recv_u.at[pair_of(g)],
            send_sem=u_ssem, recv_sem=u_rsem, device_id={"grp": peer},
        ).start()
        return carry

    lax.fori_loop(1, group_count, send_down, 0)
    lax.fori_loop(1, group_count, send_up, 0)

    def fill(pair):
        for j in (2 * pair, 2 * pair + 1):
            load_weight[j].wait()
            swap_weight(j).wait_recv()

        def one(r, carry):
            both = product(pair, r)
            partial[2 * pair, chunk_rows(r)] = both[:, :COLS]
            partial[2 * pair + 1, chunk_rows(r)] = both[:, COLS:]
            return carry

        lax.fori_loop(0, chunks, one, 0)

    def first_hop(i, carry):
        low, high = i, half + i
        pass_on(PLUS, 1, high, partial[2, chunk_rows(high)])
        pass_on(MINUS, 1, low, partial[3, chunk_rows(low)])
        return carry

    def first_sum(i, carry):
        low, high = i, half + i
        pass_on(PLUS, 1, low, partial[2, chunk_rows(low)] + arrived(PLUS, 0, low))
        pass_on(MINUS, 1, high, partial[3, chunk_rows(high)] + arrived(MINUS, 0, high))
        return carry

    def hop(s):
        def one(i, carry):
            high = lax.rem(i + half, chunks)
            pass_on(PLUS, s, high, partial[2 * s, chunk_rows(high)] + arrived(PLUS, s - 1, high))
            pass_on(MINUS, s, i, partial[2 * s + 1, chunk_rows(i)] + arrived(MINUS, s - 1, i))
            return carry

        lax.fori_loop(0, chunks, one, 0)

    fill(1)
    lax.fori_loop(0, half, first_hop, 0)
    fill(2)
    lax.fori_loop(0, half, first_sum, 0)
    fill(3)
    hop(2)
    hop(3)

    others_d = recv_d.at[pl.ds(0, CAP * (group_count - 1))]
    pltpu.make_async_copy(others_d, others_d, d_rsem).wait()

    def block_rows(n):
        return pl.ds(pl.multiple_of(n * BLOCK, BLOCK), BLOCK)

    def reduce_block(n, carry):
        rank_part[n] = lax.dot_general(
            recv_d[slot_scalar[n]], own_tokens[block_rows(n)], (((1,), (1,)), ((), ())),
            preferred_element_type=jnp.float32,
        )
        return carry

    lax.fori_loop(0, blocks, reduce_block, 0)

    def scatter_rank(k, carry):
        peer = lax.rem(t + k, tp)
        pltpu.make_async_remote_copy(
            src_ref=rank_part.at[peer], dst_ref=rank_recv.at[t],
            send_sem=r_ssem, recv_sem=r_rsem, device_id={"tp": peer},
        ).start()
        return carry

    lax.fori_loop(1, tp, scatter_rank, 0)
    rank_recv[t] = rank_part[t]
    others_r = rank_recv.at[pl.ds(0, tp - 1)]
    pltpu.make_async_copy(others_r, others_r, r_rsem).wait()
    total = jnp.sum(rank_recv[...], axis=0)
    rank_sum[...] = total
    rank_full[t] = total

    def gather_rank(k, carry):
        pltpu.make_async_remote_copy(
            src_ref=rank_sum, dst_ref=rank_full.at[t],
            send_sem=f_ssem, recv_sem=f_rsem, device_id={"tp": lax.rem(t + k, tp)},
        ).start()
        return carry

    lax.fori_loop(1, tp, gather_rank, 0)

    def last_sum(i, carry):
        high = lax.rem(i + half, chunks)
        partial[1, chunk_rows(high)] += arrived(PLUS, 3, high)
        partial[1, chunk_rows(i)] += arrived(MINUS, 3, i)
        return carry

    lax.fori_loop(0, chunks, last_sum, 0)

    others_u = recv_u.at[pl.ds(0, CAP * (group_count - 1))]
    pltpu.make_async_copy(others_u, others_u, u_rsem).wait()
    pltpu.make_async_copy(others_r, others_r, f_rsem).wait()
    offsets = lax.broadcasted_iota(jnp.int32, (BLOCK, COLS), 0)

    def finish(n, carry):
        lowrank = lax.dot_general(
            rank_full[n], recv_u[slot_scalar[n]].astype(jnp.float32), (((0,), (0,)), ((), ())),
            precision=lax.Precision.HIGHEST, preferred_element_type=jnp.float32,
        )
        value = partial[1, block_rows(n)] + adapter_scale * lowrank
        out[block_rows(n)] = jnp.where(offsets < count[n], value, 0.0).astype(out.dtype)
        return carry

    lax.fori_loop(0, blocks, finish, 0)

    def sent_far(i, carry):
        for d, r in ((PLUS, i), (MINUS, half + i)):
            data_copy(d, 0, r).wait_send()
            scale_copy(d, 0, r).wait_send()
        return carry

    lax.fori_loop(0, half, sent_far, 0)

    def sent_chunk(r, carry):
        for d in (PLUS, MINUS):
            for s in (1, 2, 3):
                data_copy(d, s, r).wait_send()
                scale_copy(d, s, r).wait_send()
        swap_tokens(r).wait_send()
        return carry

    lax.fori_loop(0, chunks, sent_chunk, 0)
    for j in range(8):
        swap_weight(j).wait_send()
    pltpu.make_async_copy(all_ids, all_ids, id_ssem).wait()
    pltpu.make_async_copy(others_d, others_d, d_ssem).wait()
    pltpu.make_async_copy(others_u, others_u, u_ssem).wait()
    pltpu.make_async_copy(others_r, others_r, r_ssem).wait()
    pltpu.make_async_copy(others_r, others_r, f_ssem).wait()


def body(tokens, base_weight, down_tables, up_tables, block_owner, block_local, block_count):
    group_count = lax.axis_size("grp")
    tp = lax.axis_size("tp")
    rows, feats = tokens.shape
    adapters = down_tables.shape[0]
    chunks = rows // CHUNK
    blocks = rows // BLOCK
    slots = CAP * group_count
    bf16, f32, i32 = jnp.bfloat16, jnp.float32, jnp.int32
    dma = pltpu.SemaphoreType.DMA
    vmem = pltpu.VMEM
    anywhere = pl.BlockSpec(memory_space=pl.ANY)
    scalar = pl.BlockSpec(memory_space=pltpu.SMEM)
    return pl.pallas_call(
        functools.partial(kernel, group_count),
        out_shape=jax.ShapeDtypeStruct((rows, COLS), bf16),
        in_specs=[anywhere] * 4 + [scalar] * 3,
        out_specs=pl.BlockSpec(memory_space=pltpu.VMEM),
        scratch_shapes=[
            vmem((rows, feats), bf16), vmem((rows, feats), bf16),
            vmem((feats, 8 * COLS), bf16), vmem((feats, 8 * COLS), bf16),
            vmem((8, rows, COLS), f32),
            vmem((2, 4, rows, COLS), jnp.int16), vmem((2, 4, rows, COLS), jnp.int16),
            vmem((2, 4, chunks, GROUPS, COLS), f32), vmem((2, 4, chunks, GROUPS, COLS), f32),
            vmem((adapters, R, feats), bf16), vmem((adapters, R, COLS), bf16),
            vmem((slots, R, feats), bf16), vmem((slots, R, feats), bf16),
            vmem((slots, R, COLS), bf16), vmem((slots, R, COLS), bf16),
            vmem((8, 128), i32), vmem((group_count, 8, 128), i32),
            pltpu.SMEM((group_count, 128), i32), pltpu.SMEM((blocks,), i32),
            vmem((blocks, R, BLOCK), f32), vmem((tp, R, BLOCK), f32),
            vmem((R, BLOCK), f32), vmem((blocks, R, BLOCK), f32),
            dma((3,)), dma((8,)), dma((chunks,)), dma((chunks,)), dma((8,)), dma((8,)),
            dma((2, 4, chunks)), dma((2, 4, chunks)), dma((2, 4, chunks)), dma((2, 4, chunks)),
            dma, dma, dma, dma, dma, dma, dma, dma, dma, dma, dma,
        ],
        compiler_params=pltpu.CompilerParams(
            collective_id=0, has_side_effects=True, vmem_limit_bytes=56 * 2**20
        ),
    )(
        tokens, base_weight, jnp.transpose(down_tables, (0, 2, 1)), up_tables,
        block_owner[:, 0], block_local, block_count,
    )


def solution(mesh):
    placed = (
        P("grp", "tp"),
        P("tp", None),
        P("grp", "tp", None),
        P("grp", None, "tp"),
        P("grp", None),
        P("grp"),
        P("grp"),
    )
    return jax.shard_map(
        body, mesh=mesh, in_specs=placed, out_specs=P("grp", "tp"), check_vma=False
    )
```

time: 298 us -> 84.9 us (0.28)
  waiting for transfers between devices: 228 us -> 0 us
  Pallas kernels: 0 us -> 82.9 us
  blocking collectives: 18.9 us -> 0 us
  between operations: 13.5 us -> 0.01 us
  matrix products: 13 us -> 0 us
  starting transfers between devices: 10.7 us -> 0 us
  other arithmetic: 6.85 us -> 0 us
  local copies, waits for them, and re-layouts: 5.47 us -> 1.87 us
    reduce_scatter x1 -> x0, waiting for transfers between devices: 103 us -> none  [body(): lax.psum_scatter(partial_value, 'tp', scatter_dimension=1, tiled=True)]
    psum x1 -> x0, waiting for transfers between devices: 89.5 us -> none  [body(): reduced = lax.psum(reduced, 'tp')]
    pallas_call x0 -> x1, Pallas kernels: none -> 82.9 us  [body(): pl.pallas_call(functools.partial(kernel, group_count), out_shape=jax.Shap...]
    all_to_all x2 -> x0, waiting for transfers between devices: 35.6 us -> none  [the longest x1 25.2 us: body(): lax.all_to_all(down_sel, 'grp', split_axis=0, concat_axis=0, tiled=True)]
    all_to_all x1 -> x0, blocking collectives: 18.9 us -> none  [body(): lax.all_to_all(wanted_ids, 'grp', split_axis=0, concat_axis=0, tiled=True)]
    dot_general x3 -> x0, matrix products: 13 us -> none  [the longest x1 9.68 us: body(): jnp.dot(tokens, base_weight, preferred_element_type=jnp.float32)]
    all_to_all x2 -> x0, starting transfers between devices: 10.7 us -> none  [the longest x1 6.74 us: body(): lax.all_to_all(up_sel, 'grp', split_axis=0, concat_axis=0, tiled=True)]
    gather x4 -> x0, local copies, waits for them, and re-layouts: 3.97 us -> none  [the longest x1 2.2 us: body(): down_sel = jnp.take(down_tables, local_ids, axis=0)]
  transfers between devices with their start and end apart: 4 -> 0, of which waited for: 4 -> 0; matrix products, arithmetic and copies ran while one was open for 5% -> 0% of each run, Pallas kernels for 0% -> 0%
where the time goes in v1:
time: 84.9 us; the launch traced here: 84.8 us
  Pallas kernels  82.9 us (98%)
  local copies, waits for them, and re-layouts  1.87 us (2%)
    pallas_call x1, Pallas kernels, body(): pl.pallas_call(functools.partial(kernel, group_count), out_shape=jax.Shap...  82.9 us
    unnamed x1, local copies, waits for them, and re-layouts  1.87 us

profile of v1, /device:TPU:1, one launch (start us, length us, event | category | flops | bytes accessed | tf_op | source)
XLA Modules:
  0.0 84.8 jit_solution(17516827167766057864)
XLA Ops:
  0.0 82.9 %shard_map.73 = bf16[2048,128]{1,0:T(8,128)(2,1)} custom-call(bf16[2048,512]{1,0:T(8,128)(2,1)} %tokens.1, bf16[512,2048]{1,0:T(8,128)(2,1)} %weight.1, bf16[128,16,512]{2,1,0:T(8,128)(2,1)} %bitcast.2, bf16[128,16,128]{2,1,0:T(8,128)(2,1)} %up_table.1, s32[16]{0:T(128)} %bitcast.3, s32[16]{0:T(128)} %local.1, s32[16]{0:T(128)} %count.1), custom_call_target="tpu_custom_call" | custom-call | tf_op jit(solution)/shard_map/pallas_call | solution.py:363
  82.9 1.9 %copy.9 = bf16[2048,128]{1,0:T(8,128)(2,1)} copy(bf16[2048,128]{1,0:T(8,128)(2,1)} %shard_map.73) | data formatting | bytes 1048576
